TPU v7x, 256 devices: a whole 4x4x8 slice. The times are simulated.
256 devices in a mesh: seq: 64 (over z, y, x_hi), tp: 4 (over x_lo, core).
Axes of the slice: x: 4 (x_hi: 2, x_lo: 2; x = x_hi * 2 + x_lo), y: 4, z: 8, core: 2. Of those that a mesh axis runs over, the one named last changes fastest.
Arguments:
- latents: bfloat16 [16384, 5120], P('seq', 'tp'), may hold values from -6 to 6
- noise: bfloat16 [16384, 5120], P('seq', 'tp'), may hold values from -6 to 6
- tstep: int32 [256], P('seq'), may hold values from 0 to 999
- offsets: int32 [256], P('seq'), may hold values from -64 to 64, as said below
- teacher_heads: bfloat16 [16384, 2560], P('seq', 'tp'), may hold values from -6 to 6
- teacher_proj: bfloat16 [2560, 5120], P('tp', 'seq'), may hold values from -0.125 to 0.125
- queries: bfloat16 [16384, 2560], P('seq', 'tp'), may hold values from -200 to 200
- keys: bfloat16 [16384, 2560], P('seq', 'tp'), may hold values from -6 to 6
- values: bfloat16 [16384, 2560], P('seq', 'tp'), may hold values from -6 to 6
- query_tangent: bfloat16 [16384, 2560], P('seq', 'tp'), may hold values from -6 to 6
- key_tangent: bfloat16 [16384, 2560], P('seq', 'tp'), may hold values from -6 to 6
- value_tangent: bfloat16 [16384, 2560], P('seq', 'tp'), may hold values from -6 to 6
- out_proj: bfloat16 [2560, 5120], P('tp', 'seq'), may hold values from -0.125 to 0.125
Outputs:
- student_out: float32 [16384, 5120], P('seq', 'tp')
- student_tangent: float32 [16384, 5120], P('seq', 'tp')
Inputs may be any that keep to these rules, and one draw needn't show every extreme that they name: `offsets`: both ends, -64 and 64, occur in every draw.
All inputs are finite; a program needn't handle non-finite values.
Results may differ from a plain program's by a relative error of at most 0.0045.
Values may be sent and summed in bfloat16 or wider, within the bound.
No kernel may reach another device: no remote copies, remote signals or barrier semaphores. Data moves between devices by JAX's collectives and lax.ppermute only.
A program may use at most 128 MiB of HBM per device.

v0:
```python
import math
import jax
import jax.numpy as jnp
from jax import lax
from jax.sharding import PartitionSpec as P

HD = 128
WIN = 256
OFF = 64
BLK = 64
STEPS = 1000


def padded_2(block, sides, width):
    for axis, dim in sides:
        count = lax.axis_size(axis)
        forward = [(i, i + 1) for i in range(count - 1)]
        backward = [(target, source) for source, target in forward]
        low = lax.ppermute(
            lax.slice_in_dim(block, block.shape[dim] - width, None, axis=dim), axis, forward
        )
        high = lax.ppermute(lax.slice_in_dim(block, 0, width, axis=dim), axis, backward)
        block = jnp.concatenate([low, block, high], axis=dim)
    return block


def body(
    latents,
    noise,
    tstep,
    offsets,
    teacher_heads,
    teacher_proj,
    queries,
    keys,
    values,
    query_tangent,
    key_tangent,
    value_tangent,
    out_proj,
):
    tokens_here = latents.shape[0]
    width_here = queries.shape[1]
    heads_here = width_here // HD
    reach = WIN // 2 + OFF
    score_scale = 1.0 / math.sqrt(HD)
    step_time = (tstep.astype(jnp.float32) + 0.5) * (math.pi / (2 * STEPS))
    per_token = jnp.repeat(step_time, BLK)[:, None]
    cosine = jnp.cos(per_token)
    sine_t = jnp.sin(per_token)
    noisy = cosine * latents.astype(jnp.float32) + sine_t * noise.astype(jnp.float32)
    teacher_term = jnp.dot(
        teacher_heads,
        lax.all_gather(teacher_proj, "seq", axis=1, tiled=True),
        preferred_element_type=jnp.float32,
    )
    velocity = lax.psum_scatter(teacher_term, "tp", scatter_dimension=1, tiled=True)
    stacked = jnp.stack([keys, values, key_tangent, value_tangent], 0)
    padded = padded_2(stacked, (("seq", 1),), reach)
    padded = padded.reshape(4, tokens_here + 2 * reach, heads_here, HD)
    first_pos = lax.axis_index("seq") * tokens_here
    total_tokens = tokens_here * lax.axis_size("seq")
    block_count = tokens_here // BLK
    span = BLK + WIN
    block_low = offsets - WIN // 2
    starts = jnp.arange(block_count, dtype=jnp.int32) * BLK + reach + block_low

    def take_window(start_row):
        return lax.dynamic_slice_in_dim(padded, start_row, span, 1)

    windows = jax.vmap(take_window, out_axes=1)(starts)
    key_block = windows[0]
    value_block = windows[1]
    key_dot = windows[2]
    value_dot = windows[3]
    query_block = queries.reshape(block_count, BLK, heads_here, HD)
    query_dot = query_tangent.reshape(block_count, BLK, heads_here, HD)
    query_pos = first_pos + jnp.arange(tokens_here, dtype=jnp.int32).reshape(block_count, BLK)
    key_pos = first_pos + starts[:, None] - reach + jnp.arange(span, dtype=jnp.int32)[None, :]
    relative = key_pos[:, None, :] - query_pos[:, :, None]
    window_low = block_low[:, None, None]
    inside = (relative >= window_low) & (relative < window_low + WIN)
    inside = inside & ((key_pos >= 0) & (key_pos < total_tokens))[:, None, :]
    inside = inside[:, None]
    scores = (
        jnp.einsum("bqhd,bkhd->bhqk", query_block, key_block, preferred_element_type=jnp.float32)
        * score_scale
    )
    scores = jnp.where(inside, scores, -1e30)
    peak_val = jnp.max(scores, axis=-1, keepdims=True)
    expo_val = jnp.where(inside, jnp.exp(scores - peak_val), 0.0)
    weights = expo_val / jnp.sum(expo_val, axis=-1, keepdims=True)
    score_dot = jnp.einsum(
        "bqhd,bkhd->bhqk", query_dot, key_block, preferred_element_type=jnp.float32
    )
    score_dot = (
        score_dot
        + jnp.einsum("bqhd,bkhd->bhqk", query_block, key_dot, preferred_element_type=jnp.float32)
    ) * score_scale
    weight_dot = weights * (score_dot - jnp.sum(weights * score_dot, axis=-1, keepdims=True))
    weights_low = weights.astype(jnp.bfloat16)
    weight_dot_low = weight_dot.astype(jnp.bfloat16)
    attended = jnp.einsum(
        "bhqk,bkhd->bqhd", weights_low, value_block, preferred_element_type=jnp.float32
    )
    attended_tangent = jnp.einsum(
        "bhqk,bkhd->bqhd", weight_dot_low, value_block, preferred_element_type=jnp.float32
    )
    attended_tangent = attended_tangent + jnp.einsum(
        "bhqk,bkhd->bqhd", weights_low, value_dot, preferred_element_type=jnp.float32
    )
    attended = attended.astype(jnp.bfloat16).reshape(tokens_here, width_here)
    attended_tangent = attended_tangent.astype(jnp.bfloat16).reshape(tokens_here, width_here)
    branch_term = jnp.dot(
        attended,
        lax.all_gather(out_proj, "seq", axis=1, tiled=True),
        preferred_element_type=jnp.float32,
    )
    tangent_term = jnp.dot(
        attended_tangent,
        lax.all_gather(out_proj, "seq", axis=1, tiled=True),
        preferred_element_type=jnp.float32,
    )
    branch, branch_tangent = (
        lax.psum_scatter(branch_term, "tp", scatter_dimension=1, tiled=True),
        lax.psum_scatter(tangent_term, "tp", scatter_dimension=1, tiled=True),
    )
    student_out = cosine * noisy - sine_t * branch
    student_tangent = (
        -sine_t * noisy + cosine * velocity - cosine * branch - sine_t * branch_tangent
    )
    return (student_out, student_tangent)


def solution(mesh):
    return jax.shard_map(
        body,
        mesh=mesh,
        in_specs=(
            P("seq", "tp"),
            P("seq", "tp"),
            P("seq"),
            P("seq"),
            P("seq", "tp"),
            P("tp", "seq"),
            P("seq", "tp"),
            P("seq", "tp"),
            P("seq", "tp"),
            P("seq", "tp"),
            P("seq", "tp"),
            P("seq", "tp"),
            P("tp", "seq"),
        ),
        out_specs=(P("seq", "tp"), P("seq", "tp")),
        check_vma=False,
    )
```

profile of v0, /device:TPU:1, one launch (start us, length us, event | category | flops | bytes accessed | tf_op | source)
XLA Modules:
  0.0 496.5 jit_solution(10031335165689679332)
XLA Ops:
  15.4 5.6 %collective-permute-start = (bf16[4,192,640]{2,1,0:T(8,128)(2,1)}, bf16[4,192,640]{2,1,0:T(8,128)(2,1)S(1)}, u32[]{:S(2)}, u32[]{:S(2)}) collective-permute-start(bf16[4,192,640]{2,1,0:T(8,128)(2,1)} %copy.36), channel_id=1, source_target_pairs={{0,4},{4,8},{8,12},{12,16},{16,20},{20,24},{24,28},{28,32},{32,36}... | collective-permute-start | bytes 2949128 | tf_op jit(solution)/shard_map/ppermute | solution.py:19
  26.1 37.4 %collective-permute-done = bf16[4,192,640]{2,1,0:T(8,128)(2,1)S(1)} collective-permute-done((bf16[4,192,640]{2,1,0:T(8,128)(2,1)}, bf16[4,192,640]{2,1,0:T(8,128)(2,1)S(1)}, u32[]{:S(2)}, u32[]{:S(2)}) %collective-permute-start) | collective-permute-done | bytes 983072 | tf_op jit(solution)/shard_map/ppermute | solution.py:19
  67.0 5.7 %pad_maximum_fusion = bf16[4,640,640]{1,2,0:T(8,128)(2,1)} fusion(bf16[4,192,640]{1,2,0:T(8,128)(2,1)S(1)} %copy.39, bf16[1,256,640]{1,2,0:T(8,128)(2,1)} %bitcast.93, bf16[1,256,640]{1,2,0:T(8,128)(2,1)} %bitcast.91, bf16[1,256,640]{1,2,0:T(8,128)(2,1)} %bitcast.89, bf16[1,256,640]{1,2,0:T(8,128)(2,1)S(1)} %bitcast.87, bf16[4,192,640]{1,2,0:T(8,128)(2,1)S(1)} %copy.38), kind=kLoop, calls=%fused_computation.4 | loop fusion | flops 19660800 | bytes 6553600 | tf_op jit(solution)/shard_map/concatenate | solution.py:23
  72.7 41.2 %while.1 = (s32[]{:T(128)}, bf16[4,640,5,128]{1,3,2,0:T(8,128)(2,1)}, s32[4,4]{1,0:T(4,128)S(1)}, bf16[4,4,320,5,128]{4,2,3,0,1:T(8,128)(2,1)}, s32[]{:T(128)}) while((s32[]{:T(128)}, bf16[4,640,5,128]{1,3,2,0:T(8,128)(2,1)}, s32[4,4]{1,0:T(4,128)S(1)}, bf16[4,4,320,5,128]{4,2,3,0,1:T(8,128)(2,1)}, s32[]{:T(128)}) %tuple.43), condition=%wide.while_cond, body=%wide.while_body.sunk | while | flops 2 | bytes 9831021 | solution.py:69
  73.3 4.7 constant_dynamic-slice_fusion.5
  78.0 3.5 copy.77
  83.6 4.7 constant_dynamic-slice_fusion.5
  88.3 3.5 copy.77
  93.9 4.7 constant_dynamic-slice_fusion.5
  98.6 3.5 copy.77
  104.2 4.5 constant_dynamic-slice_fusion.5
  108.8 3.5 copy.77
  113.9 3.8 fusion.40
  117.6 2.6 fusion.14
  120.5 46.9 %all-gather.3.cloned.1.call-done = bf16[640,5120]{0,1:T(8,128)(2,1)} async-done(((bf16[640,80]{0,1:T(8,128)(2,1)}), bf16[640,5120]{0,1:T(8,128)(2,1)}) %all-gather.3.cloned.1.call-update) | async-done | bytes 6553616 | tf_op jit(solution)/shard_map/all_gather | solution.py:116
  167.3 7.4 %fusion.28 = f32[256,5120]{1,0:T(8,128)} fusion(bf16[640,5120]{0,1:T(8,128)(2,1)} %all-gather.3.cloned.1.call-done, bf16[32,8,5,128]{3,2,1,0:T(8,128)(2,1)S(1)} %bitcast.94), kind=kOutput, calls=%fused_computation.47 | convolution fusion | flops 1677721600 | bytes 12124160 | tf_op jit(solution)/shard_map/dot_general | solution.py:114
  178.4 2.7 fusion.5
  185.0 4.6 fusion.25
  189.7 116.9 %all-gather.5.cloned.1.call-done = bf16[640,5120]{0,1:T(8,128)(2,1)} async-done(((bf16[640,80]{0,1:T(8,128)(2,1)}), bf16[640,5120]{0,1:T(8,128)(2,1)}) %all-gather.5.cloned.1.call-update) | async-done | bytes 6553616 | tf_op jit(solution)/shard_map/all_gather | solution.py:54
  306.5 7.3 %fusion.45 = f32[256,5120]{1,0:T(8,128)} fusion(bf16[256,640]{1,0:T(8,128)(2,1)S(1)} %copy-done, bf16[640,5120]{0,1:T(8,128)(2,1)} %all-gather.5.cloned.1.call-done), kind=kOutput, calls=%fused_computation.70 | convolution fusion | flops 1677721600 | bytes 12124160 | tf_op jit(solution)/shard_map/dot_general | solution.py:52
  314.9 51.1 %reduce-scatter.4.cloned.1.call-done = f32[256,1280]{1,0:T(8,128)} async-done(((f32[256,5120]{1,0:T(8,128)}), f32[256,1280]{1,0:T(8,128)}) %reduce-scatter.4.cloned.1.call-update) | async-done | bytes 1310736 | tf_op jit(solution)/shard_map/reduce_scatter | solution.py:125
  366.0 59.8 %reduce-scatter.8.cloned.1.call-done = f32[256,1280]{1,0:T(8,128)} async-done(((f32[256,5120]{1,0:T(8,128)}), f32[256,1280]{1,0:T(8,128)}) %reduce-scatter.8.cloned.1.call-update) | async-done | bytes 1310736 | tf_op jit(solution)/shard_map/reduce_scatter | solution.py:126
  425.9 59.8 %reduce-scatter.6.cloned.1.call-done = f32[256,1280]{1,0:T(8,128)} async-done(((f32[256,5120]{1,0:T(8,128)}), f32[256,1280]{1,0:T(8,128)}) %reduce-scatter.6.cloned.1.call-update) | async-done | bytes 1310736 | tf_op jit(solution)/shard_map/reduce_scatter | solution.py:57
  485.7 4.3 multiply_subtract_fusion
  (94 shorter events, 34.1 us)
Async XLA Ops:
  7.2 299.4 %copy-start = (bf16[256,640]{1,0:T(8,128)(2,1)S(1)}, bf16[256,640]{1,0:T(8,128)(2,1)}, u32[]{:S(2)}) copy-start(bf16[256,640]{1,0:T(8,128)(2,1)} %param.17) | copy-start | bytes 983044
  7.2 5.1 %copy-start.7 = (bf16[256,640]{1,0:T(8,128)(2,1)S(1)}, bf16[256,640]{1,0:T(8,128)(2,1)}, u32[]{:S(2)}) copy-start(bf16[256,640]{1,0:T(8,128)(2,1)} %param.24) | copy-start | bytes 983044
  7.2 160.1 %all-gather.3.cloned.1.call-start = ((), (), s32[]{:S(2)}) async-start(), calls=%async_computation.3 | async-start | bytes 6656000 | tf_op jit(solution)/shard_map/all_gather | solution.py:116
  7.9 298.6 %all-gather.5.cloned.1.call-start = ((), (), s32[]{:S(2)}) async-start(), calls=%async_computation.5 | async-start | bytes 6656000 | tf_op jit(solution)/shard_map/all_gather | solution.py:54
  8.7 357.4 %reduce-scatter.4.cloned.1.call-start = ((), (), s32[]{:S(2)}) async-start(), calls=%async_computation.4 | async-start | bytes 6553600 | tf_op jit(solution)/shard_map/reduce_scatter | solution.py:125
  11.0 1.5 copy-start.1
  12.3 0.7 copy-start.2
  12.5 0.7 copy-start.3
  14.0 9.8 %copy-start.10 = (s32[4]{0:T(128)S(1)}, s32[4]{0:T(128)}, u32[]{:S(2)}) copy-start(s32[4]{0:T(128)} %param.16) | copy-start | bytes 52
  15.4 8.5 %copy-start.8 = (bf16[256,640]{1,0:T(8,128)(2,1)S(1)}, bf16[256,640]{1,0:T(8,128)(2,1)}, u32[]{:S(2)}) copy-start(bf16[256,640]{1,0:T(8,128)(2,1)} %param.19) | copy-start | bytes 983044
  15.4 48.1 %collective-permute-start = (bf16[4,192,640]{2,1,0:T(8,128)(2,1)}, bf16[4,192,640]{2,1,0:T(8,128)(2,1)S(1)}, u32[]{:S(2)}, u32[]{:S(2)}) collective-permute-start(bf16[4,192,640]{2,1,0:T(8,128)(2,1)} %copy.36), channel_id=1, source_target_pairs={{0,4},{4,8},{8,12},{12,16},{16,20},{20,24},{24,28},{28,32},{32,36}... | collective-permute-start | bytes 2949128 | tf_op jit(solution)/shard_map/ppermute | solution.py:19
  22.4 43.1 %collective-permute-start.1 = (bf16[4,192,640]{2,1,0:T(8,128)(2,1)}, bf16[4,192,640]{2,1,0:T(8,128)(2,1)}, u32[]{:S(2)}, u32[]{:S(2)}) collective-permute-start(bf16[4,192,640]{2,1,0:T(8,128)(2,1)} %copy.37), channel_id=1, source_target_pairs={{4,0},{8,4},{12,8},{16,12},{20,16},{24,20},{28,24},{32,28},{36,32}... | collective-permute-start | bytes 2949128 | tf_op jit(solution)/shard_map/ppermute | solution.py:22
  72.7 41.2 %copy-start.6 = (bf16[4,64,5,128]{3,2,1,0:T(8,128)(2,1)S(1)}, bf16[4,64,5,128]{3,2,1,0:T(8,128)(2,1)}, u32[]{:S(2)}) copy-start(bf16[4,64,5,128]{3,2,1,0:T(8,128)(2,1)} %reshape.106) | copy-start | bytes 983044
  174.7 1.0 copy-start.9
  174.7 251.1 %reduce-scatter.8.cloned.1.call-start = ((), (), s32[]{:S(2)}) async-start(), calls=%async_computation.7 | async-start | bytes 6553600 | tf_op jit(solution)/shard_map/reduce_scatter | solution.py:126
  176.1 5.0 %slice-start.2 = ((s8[6553600]{0:T(1024)(128)(4,1)}), s8[4194304]{0:T(1024)(128)(4,1)S(1)}, s32[]{:S(2)}) async-start(s8[6553600]{0:T(1024)(128)(4,1)} %bitcast.100), calls=%async_computation.10 | async-start | bytes 8388608
  178.3 3.4 slice-start.3
  178.3 3.4 copy-start.12
  181.8 2.2 slice-start
  182.8 2.2 slice-start.1
  189.6 296.1 %reduce-scatter.6.cloned.1.call-start = ((), (), s32[]{:S(2)}) async-start(), calls=%async_computation.6 | async-start | bytes 6553600 | tf_op jit(solution)/shard_map/reduce_scatter | solution.py:57
  313.9 0.7 copy-start.11
  313.9 171.8 %copy-start.4 = (bf16[256,1280]{1,0:T(8,128)(2,1)S(1)}, bf16[256,1280]{1,0:T(8,128)(2,1)}, u32[]{:S(2)}) copy-start(bf16[256,1280]{1,0:T(8,128)(2,1)} %param.14) | copy-start | bytes 1966084
  313.9 171.8 %copy-start.5 = (bf16[256,1280]{1,0:T(8,128)(2,1)S(1)}, bf16[256,1280]{1,0:T(8,128)(2,1)}, u32[]{:S(2)}) copy-start(bf16[256,1280]{1,0:T(8,128)(2,1)} %param.13) | copy-start | bytes 1966084
Sparse Core Ops, SparseCore 0:
  11.5 155.8 all-gather.2
  170.8 135.6 all-gather.4
  309.1 56.9 reduce-scatter.3
  368.5 57.3 reduce-scatter.7
  428.3 57.3 reduce-scatter.5
where the time goes:
time: 497 us
  waiting for transfers between devices  375 us (75%)
  local copies, waits for them, and re-layouts  57 us (11%)
  matrix products  32.1 us (6%)
  between operations  14 us (3%)
  other arithmetic  11.3 us (2%)
  starting transfers between devices  7.3 us (1%)
    all_gather x1, waiting for transfers between devices, body(): lax.all_gather(teacher_proj, 'seq', axis=1, tiled=True)  117 us
    reduce_scatter x1, waiting for transfers between devices, body(): lax.psum_scatter(tangent_term, 'tp', scatter_dimension=1, tiled=True)  59.8 us
    reduce_scatter x1, waiting for transfers between devices, body(): lax.psum_scatter(teacher_term, 'tp', scatter_dimension=1, tiled=True)  59.8 us
    reduce_scatter x1, waiting for transfers between devices, body(): lax.psum_scatter(branch_term, 'tp', scatter_dimension=1, tiled=True)  51.1 us
    all_gather x1, waiting for transfers between devices, body(): lax.all_gather(out_proj, 'seq', axis=1, tiled=True)  46.9 us
    gather x20, local copies, waits for them, and re-layouts  41.1 us
    ppermute x1, waiting for transfers between devices, padded_2(): lax.ppermute(lax.slice_in_dim(block, block.shape[dim] - width, None, axis...  37.4 us
  transfers between devices with their start and end apart: 7, of which 7 were waited for; matrix products, arithmetic and copies ran while one was open for 19% of the time, Pallas kernels for 0%

commit v1 on v0

--- a/solution.py
+++ b/solution.py
@@ -9,6 +9,11 @@
 OFF = 64
 BLK = 64
 STEPS = 1000
+
+
+def swapped_in(value, mesh_axis, dim):
+    sent = jnp.stack([value] * lax.axis_size(mesh_axis))
+    return jnp.concatenate(lax.all_to_all(sent, mesh_axis, 0, 0), axis=dim)
 
 
 def padded_2(block, sides, width):
@@ -50,9 +55,7 @@
     sine_t = jnp.sin(per_token)
     noisy = cosine * latents.astype(jnp.float32) + sine_t * noise.astype(jnp.float32)
     teacher_term = jnp.dot(
-        teacher_heads,
-        lax.all_gather(teacher_proj, "seq", axis=1, tiled=True),
-        preferred_element_type=jnp.float32,
+        teacher_heads, swapped_in(teacher_proj, "seq", 1), preferred_element_type=jnp.float32
     )
     velocity = lax.psum_scatter(teacher_term, "tp", scatter_dimension=1, tiled=True)
     stacked = jnp.stack([keys, values, key_tangent, value_tangent], 0)

time: 497 us -> 433 us (0.87)
  waiting for transfers between devices: 375 us -> 299 us
  starting transfers between devices: 7.3 us -> 15.3 us
    all_to_all x0 -> x1, waiting for transfers between devices: none -> 128 us  [swapped_in(): return jnp.concatenate(lax.all_to_all(sent, mesh_axis, 0, 0), axis=dim)]
    all_gather x1 -> x0, waiting for transfers between devices: 117 us -> none  [body(): lax.all_gather(teacher_proj, 'seq', axis=1, tiled=True)]
    reduce_scatter x1, waiting for transfers between devices: 51.1 us -> 0.01 us  [body(): lax.psum_scatter(branch_term, 'tp', scatter_dimension=1, tiled=True)]
    reduce_scatter x1, waiting for transfers between devices: 59.8 us -> 18.6 us  [body(): lax.psum_scatter(tangent_term, 'tp', scatter_dimension=1, tiled=True)]
    all_to_all x0 -> x1, starting transfers between devices: none -> 8.23 us  [swapped_in(): return jnp.concatenate(lax.all_to_all(sent, mesh_axis, 0, 0), axis=dim)]
    all_gather x1, waiting for transfers between devices: 46.9 us -> 52.3 us  [body(): lax.all_gather(out_proj, 'seq', axis=1, tiled=True)]
  transfers between devices with their start and end apart: 7 -> 7, of which waited for: 7 -> 6; matrix products, arithmetic and copies ran while one was open for 19% -> 20% of each run, Pallas kernels for 0% -> 0%
where the time goes in v1:
time: 433 us; the launch traced here: 432 us
  waiting for transfers between devices  299 us (69%)
  local copies, waits for them, and re-layouts  60.4 us (14%)
  matrix products  32.3 us (7%)
  starting transfers between devices  15.3 us (4%)
  between operations  14 us (3%)
  other arithmetic  11.4 us (3%)
    all_to_all x1, waiting for transfers between devices, swapped_in(): return jnp.concatenate(lax.all_to_all(sent, mesh_axis, 0, 0), axis=dim)  128 us
    reduce_scatter x1, waiting for transfers between devices, body(): lax.psum_scatter(teacher_term, 'tp', scatter_dimension=1, tiled=True)  60.5 us
    all_gather x1, waiting for transfers between devices, body(): lax.all_gather(out_proj, 'seq', axis=1, tiled=True)  52.3 us
    gather x20, local copies, waits for them, and re-layouts  41.1 us
    ppermute x1, waiting for transfers between devices, padded_2(): lax.ppermute(lax.slice_in_dim(block, block.shape[dim] - width, None, axis...  37.4 us
    reduce_scatter x1, waiting for transfers between devices, body(): lax.psum_scatter(tangent_term, 'tp', scatter_dimension=1, tiled=True)  18.6 us
  transfers between devices with their start and end apart: 7, of which 6 were waited for; matrix products, arithmetic and copies ran while one was open for 20% of the time, Pallas kernels for 0%

profile of v1, /device:TPU:1, one launch (start us, length us, event | category | flops | bytes accessed | tf_op | source)
XLA Modules:
  0.0 432.1 jit_solution(16459258443561854225)
XLA Ops:
  14.6 5.6 %collective-permute-start = (bf16[4,192,640]{2,1,0:T(8,128)(2,1)}, bf16[4,192,640]{2,1,0:T(8,128)(2,1)S(1)}, u32[]{:S(2)}, u32[]{:S(2)}) collective-permute-start(bf16[4,192,640]{2,1,0:T(8,128)(2,1)} %copy.37), channel_id=1, source_target_pairs={{0,4},{4,8},{8,12},{12,16},{16,20},{20,24},{24,28},{28,32},{32,36}... | collective-permute-start | bytes 2949128 | tf_op jit(solution)/shard_map/ppermute | solution.py:24
  25.3 37.4 %collective-permute-done = bf16[4,192,640]{2,1,0:T(8,128)(2,1)S(1)} collective-permute-done((bf16[4,192,640]{2,1,0:T(8,128)(2,1)}, bf16[4,192,640]{2,1,0:T(8,128)(2,1)S(1)}, u32[]{:S(2)}, u32[]{:S(2)}) %collective-permute-start) | collective-permute-done | bytes 983072 | tf_op jit(solution)/shard_map/ppermute | solution.py:24
  66.3 5.7 %pad_maximum_fusion = bf16[4,640,640]{1,2,0:T(8,128)(2,1)} fusion(bf16[4,192,640]{1,2,0:T(8,128)(2,1)S(1)} %copy.40, bf16[1,256,640]{1,2,0:T(8,128)(2,1)} %bitcast.96, bf16[1,256,640]{1,2,0:T(8,128)(2,1)} %bitcast.94, bf16[1,256,640]{1,2,0:T(8,128)(2,1)} %bitcast.92, bf16[1,256,640]{1,2,0:T(8,128)(2,1)S(1)} %bitcast.90, bf16[4,192,640]{1,2,0:T(8,128)(2,1)S(1)} %copy.39), kind=kLoop, calls=%fused_computation.4 | loop fusion | flops 19660800 | bytes 6553600 | tf_op jit(solution)/shard_map/concatenate | solution.py:28
  72.0 41.2 %while.1 = (s32[]{:T(128)}, bf16[4,640,5,128]{1,3,2,0:T(8,128)(2,1)}, s32[4,4]{1,0:T(4,128)S(1)}, bf16[4,4,320,5,128]{4,2,3,0,1:T(8,128)(2,1)}, s32[]{:T(128)}) while((s32[]{:T(128)}, bf16[4,640,5,128]{1,3,2,0:T(8,128)(2,1)}, s32[4,4]{1,0:T(4,128)S(1)}, bf16[4,4,320,5,128]{4,2,3,0,1:T(8,128)(2,1)}, s32[]{:T(128)}) %tuple.41), condition=%wide.while_cond, body=%wide.while_body.sunk | while | flops 2 | bytes 9831021 | solution.py:72
  72.6 4.7 %constant_dynamic-slice_fusion.5 = bf16[4,320,5,128]{1,3,2,0:T(8,128)(2,1)} fusion(bf16[4,640,5,128]{1,3,2,0:T(8,128)(2,1)} %get-tuple-element.76, s32[]{:T(128)} %bitcast.83), kind=kLoop, calls=%fused_computation.2.clone.1 | loop fusion | bytes 3276804 | tf_op jit(solution)/shard_map/vmap()/gather
  77.3 3.5 copy.78
  82.9 4.7 %constant_dynamic-slice_fusion.5 = bf16[4,320,5,128]{1,3,2,0:T(8,128)(2,1)} fusion(bf16[4,640,5,128]{1,3,2,0:T(8,128)(2,1)} %get-tuple-element.76, s32[]{:T(128)} %bitcast.83), kind=kLoop, calls=%fused_computation.2.clone.1 | loop fusion | bytes 3276804 | tf_op jit(solution)/shard_map/vmap()/gather
  87.6 3.5 copy.78
  93.2 4.7 %constant_dynamic-slice_fusion.5 = bf16[4,320,5,128]{1,3,2,0:T(8,128)(2,1)} fusion(bf16[4,640,5,128]{1,3,2,0:T(8,128)(2,1)} %get-tuple-element.76, s32[]{:T(128)} %bitcast.83), kind=kLoop, calls=%fused_computation.2.clone.1 | loop fusion | bytes 3276804 | tf_op jit(solution)/shard_map/vmap()/gather
  97.9 3.5 copy.78
  103.6 4.5 %constant_dynamic-slice_fusion.5 = bf16[4,320,5,128]{1,3,2,0:T(8,128)(2,1)} fusion(bf16[4,640,5,128]{1,3,2,0:T(8,128)(2,1)} %get-tuple-element.76, s32[]{:T(128)} %bitcast.83), kind=kLoop, calls=%fused_computation.2.clone.1 | loop fusion | bytes 3276804 | tf_op jit(solution)/shard_map/vmap()/gather
  108.1 3.5 copy.78
  113.2 3.7 fusion.40
  119.7 52.3 %all-gather.2.cloned.1.call-done = bf16[640,5120]{0,1:T(8,128)(2,1)} async-done(((bf16[640,80]{0,1:T(8,128)(2,1)}), bf16[640,5120]{0,1:T(8,128)(2,1)}) %all-gather.2.cloned.1.call-update) | async-done | bytes 6553616 | tf_op jit(solution)/shard_map/all_gather | solution.py:119
  172.0 7.5 %fusion.28 = f32[256,5120]{1,0:T(8,128)} fusion(bf16[640,5120]{0,1:T(8,128)(2,1)} %all-gather.2.cloned.1.call-done, bf16[32,8,5,128]{3,2,1,0:T(8,128)(2,1)S(1)} %bitcast.97), kind=kOutput, calls=%fused_computation.47 | convolution fusion | flops 1677721600 | bytes 12124160 | tf_op jit(solution)/shard_map/dot_general | solution.py:117
  180.4 3.3 stack.17
  183.7 8.2 %all-to-all-start = ((bf16[64,640,80]{1,2,0:T(8,128)(2,1)}), bf16[64,640,80]{1,2,0:T(8,128)(2,1)}, u32[]{:S(2)}, u32[]{:S(2)}) async-start(bf16[64,640,80]{1,2,0:T(8,128)(2,1)} %stack.17), calls=%async_computation.1 | async-start | bytes 13107200 | tf_op jit(solution)/shard_map/all_to_all | solution.py:16
  194.7 2.7 fusion.5
  201.3 4.6 %fusion.25 = f32[256,5120]{1,0:T(8,128)} fusion(bf16[640,5120]{0,1:T(8,128)(2,1)S(1)} %bitcast.88, bf16[32,8,5,128]{3,2,1,0:T(8,128)(2,1)S(1)} %bitcast.98), kind=kOutput, calls=%fused_computation.44 | convolution fusion | flops 1677721600 | bytes 12124160 | tf_op jit(solution)/shard_map/dot_general | solution.py:122
  205.9 127.8 %all-to-all-done = bf16[64,640,80]{1,2,0:T(8,128)(2,1)} async-done(((bf16[64,640,80]{1,2,0:T(8,128)(2,1)}), bf16[64,640,80]{1,2,0:T(8,128)(2,1)}, u32[]{:S(2)}, u32[]{:S(2)}) %all-to-all-start) | async-done | bytes 6553632 | tf_op jit(solution)/shard_map/all_to_all | solution.py:16
  333.7 7.4 %fusion.45 = f32[256,5120]{1,0:T(8,128)} fusion(bf16[256,640]{1,0:T(8,128)(2,1)S(1)} %copy-done, bf16[640,5120]{0,1:T(8,128)(2,1)} %bitcast.12), kind=kOutput, calls=%fused_computation.70 | convolution fusion | flops 1677721600 | bytes 12124160 | tf_op jit(solution)/shard_map/dot_general | solution.py:57
  342.1 18.6 %reduce-scatter.8.cloned.1.call-done = f32[256,1280]{1,0:T(8,128)} async-done(((f32[256,5120]{1,0:T(8,128)}), f32[256,1280]{1,0:T(8,128)}) %reduce-scatter.8.cloned.1.call-update) | async-done | bytes 1310736 | tf_op jit(solution)/shard_map/reduce_scatter | solution.py:129
  360.7 60.5 %reduce-scatter.6.cloned.1.call-done = f32[256,1280]{1,0:T(8,128)} async-done(((f32[256,5120]{1,0:T(8,128)}), f32[256,1280]{1,0:T(8,128)}) %reduce-scatter.6.cloned.1.call-update) | async-done | bytes 1310736 | tf_op jit(solution)/shard_map/reduce_scatter | solution.py:60
  421.2 4.3 %multiply_subtract_fusion = (f32[256,1280]{1,0:T(8,128)}, f32[256,1280]{1,0:T(8,128)}) fusion(f32[256,1280]{1,0:T(8,128)} %reduce-scatter.8.cloned.1.call-done, f32[256,1280]{1,0:T(8,128)} %reduce-scatter.4.cloned.1.call-done, f32[256,1280]{1,0:T(8,128)} %reduce-scatter.6.cloned.1.call-done, bf16[256,1280]{1,0:T(8,128)(2,1)S(1)} %copy-done.4, ...), kind=kLoop, calls=%fused_computation.25 | loop fusion | flops 4915200 | bytes 7867392 | tf_op jit(solution)/shard_map/sub | solution.py:133
  (96 shorter events, 35.9 us)
Async XLA Ops:
  7.2 326.6 %copy-start = (bf16[256,640]{1,0:T(8,128)(2,1)S(1)}, bf16[256,640]{1,0:T(8,128)(2,1)}, u32[]{:S(2)}) copy-start(bf16[256,640]{1,0:T(8,128)(2,1)} %param.17) | copy-start | bytes 983044
  7.2 4.4 %copy-start.7 = (bf16[256,640]{1,0:T(8,128)(2,1)S(1)}, bf16[256,640]{1,0:T(8,128)(2,1)}, u32[]{:S(2)}) copy-start(bf16[256,640]{1,0:T(8,128)(2,1)} %param.24) | copy-start | bytes 983044
  7.2 164.8 %all-gather.2.cloned.1.call-start = ((), (), s32[]{:S(2)}) async-start(), calls=%async_computation.4 | async-start | bytes 6656000 | tf_op jit(solution)/shard_map/all_gather | solution.py:119
  7.9 334.2 %reduce-scatter.4.cloned.1.call-start = ((), (), s32[]{:S(2)}) async-start(), calls=%async_computation.5 | async-start | bytes 6553600 | tf_op jit(solution)/shard_map/reduce_scatter | solution.py:128
  10.3 1.5 copy-start.1
  11.5 0.7 copy-start.2
  11.7 0.7 copy-start.3
  13.2 9.8 %copy-start.11 = (s32[4]{0:T(128)S(1)}, s32[4]{0:T(128)}, u32[]{:S(2)}) copy-start(s32[4]{0:T(128)} %param.16) | copy-start | bytes 52
  14.6 8.5 %copy-start.8 = (bf16[256,640]{1,0:T(8,128)(2,1)S(1)}, bf16[256,640]{1,0:T(8,128)(2,1)}, u32[]{:S(2)}) copy-start(bf16[256,640]{1,0:T(8,128)(2,1)} %param.19) | copy-start | bytes 983044
  14.6 48.1 %collective-permute-start = (bf16[4,192,640]{2,1,0:T(8,128)(2,1)}, bf16[4,192,640]{2,1,0:T(8,128)(2,1)S(1)}, u32[]{:S(2)}, u32[]{:S(2)}) collective-permute-start(bf16[4,192,640]{2,1,0:T(8,128)(2,1)} %copy.37), channel_id=1, source_target_pairs={{0,4},{4,8},{8,12},{12,16},{16,20},{20,24},{24,28},{28,32},{32,36}... | collective-permute-start | bytes 2949128 | tf_op jit(solution)/shard_map/ppermute | solution.py:24
  21.6 43.1 %collective-permute-start.1 = (bf16[4,192,640]{2,1,0:T(8,128)(2,1)}, bf16[4,192,640]{2,1,0:T(8,128)(2,1)}, u32[]{:S(2)}, u32[]{:S(2)}) collective-permute-start(bf16[4,192,640]{2,1,0:T(8,128)(2,1)} %copy.38), channel_id=1, source_target_pairs={{4,0},{8,4},{12,8},{16,12},{20,16},{24,20},{28,24},{32,28},{36,32}... | collective-permute-start | bytes 2949128 | tf_op jit(solution)/shard_map/ppermute | solution.py:27
  72.0 41.2 %copy-start.6 = (bf16[4,64,5,128]{3,2,1,0:T(8,128)(2,1)S(1)}, bf16[4,64,5,128]{3,2,1,0:T(8,128)(2,1)}, u32[]{:S(2)}) copy-start(bf16[4,64,5,128]{3,2,1,0:T(8,128)(2,1)} %reshape.114) | copy-start | bytes 983044
  179.5 0.9 copy-start.10
  183.7 8.3 %copy-start.9 = (bf16[256,640]{1,0:T(8,128)(2,1)S(1)}, bf16[256,640]{1,0:T(8,128)(2,1)}, u32[]{:S(2)}) copy-start(bf16[256,640]{1,0:T(8,128)(2,1)} %param.22) | copy-start | bytes 983044
  183.7 150.1 %all-to-all-start = ((bf16[64,640,80]{1,2,0:T(8,128)(2,1)}), bf16[64,640,80]{1,2,0:T(8,128)(2,1)}, u32[]{:S(2)}, u32[]{:S(2)}) async-start(bf16[64,640,80]{1,2,0:T(8,128)(2,1)} %stack.17), calls=%async_computation.1 | async-start | bytes 13107200 | tf_op jit(solution)/shard_map/all_to_all | solution.py:16
  191.9 168.8 %reduce-scatter.8.cloned.1.call-start = ((), (), s32[]{:S(2)}) async-start(), calls=%async_computation.7 | async-start | bytes 6553600 | tf_op jit(solution)/shard_map/reduce_scatter | solution.py:129
  192.3 5.1 %slice-start.2 = ((s8[6553600]{0:T(1024)(128)(4,1)}), s8[4194304]{0:T(1024)(128)(4,1)S(1)}, s32[]{:S(2)}) async-start(s8[6553600]{0:T(1024)(128)(4,1)} %bitcast.103), calls=%async_computation.10 | async-start | bytes 8388608
  194.6 3.4 slice-start.3
  194.6 3.4 copy-start.13
  198.1 2.2 slice-start
  199.1 2.2 slice-start.1
  205.9 215.3 %reduce-scatter.6.cloned.1.call-start = ((), (), s32[]{:S(2)}) async-start(), calls=%async_computation.6 | async-start | bytes 6553600 | tf_op jit(solution)/shard_map/reduce_scatter | solution.py:60
  341.1 80.1 %copy-start.4 = (bf16[256,1280]{1,0:T(8,128)(2,1)S(1)}, bf16[256,1280]{1,0:T(8,128)(2,1)}, u32[]{:S(2)}) copy-start(bf16[256,1280]{1,0:T(8,128)(2,1)} %param.14) | copy-start | bytes 1966084
  341.1 80.1 %copy-start.5 = (bf16[256,1280]{1,0:T(8,128)(2,1)S(1)}, bf16[256,1280]{1,0:T(8,128)(2,1)}, u32[]{:S(2)}) copy-start(bf16[256,1280]{1,0:T(8,128)(2,1)} %param.13) | copy-start | bytes 1966084
  (1 other events, 0.7 us)
Sparse Core Ops, SparseCore 0:
  11.5 160.4 all-gather.1
  179.6 106.2 reduce-scatter.3
  288.4 72.2 reduce-scatter.7
  363.2 58.0 reduce-scatter.5
